TPU v7x, 32 devices: a whole 2x2x4 slice. The times are simulated.
32 devices in a mesh: wide: 8 (over y, x, core), narrow: 4 (over z).
Axes of the slice: x: 2, y: 2, z: 4, core: 2. Of those that a mesh axis runs over, the one named last changes fastest.
Arguments:
- pooled: bfloat16 [16384, 1024], P(('wide', 'narrow')), may hold values from -6 to 6
- cotangent: bfloat16 [16384, 512], P(('wide', 'narrow')), may hold values from -6 to 6
- w_first: bfloat16 [1024, 1024], P('narrow'), may hold values from -0.1875 to 0.1875
- b_first: float32 [1024], replicated, may hold values from -5 to 5
- w_second: bfloat16 [1024, 512], P('narrow'), may hold values from -0.1875 to 0.1875
- counts: bfloat16 [8, 64, 16384], P(None, 'narrow', 'wide'), may hold values from 0 to 3, as said below
- row_ids: int32 [8, 64], P(None, 'narrow'), may hold values from 0 to 63, as said below
- table: float32 [8, 256, 128], P(None, 'narrow'), may hold values from -6 to 6
- accum: float32 [8, 256, 128], P(None, 'narrow'), may hold values from 0.1 to 10
Outputs:
- new_table: float32 [8, 256, 128], P(None, 'narrow')
- new_accum: float32 [8, 256, 128], P(None, 'narrow')
Inputs may be any that keep to these rules, and one draw needn't show every extreme that they name: `counts`: each entry is zero where the sample does not look up the active row, else a positive lookup weight. `row_ids`: for each table, the 16 ids of one owner (slots j * 16 to (j + 1) * 16 - 1) are distinct.
All inputs are finite; a program needn't handle non-finite values.
Results may differ from a plain program's by a relative error of at most 0.0038.
Values may be sent and summed in bfloat16 or wider, within the bound.
A program may use at most 128 MiB of HBM per device.

v0:
```python
import functools
import math

import jax
import jax.numpy as jnp
from jax import lax
from jax.experimental import pallas as pl
from jax.experimental.pallas import tpu as pltpu
from jax.sharding import PartitionSpec as P

MESH = pl.DeviceIdType.MESH
clip_factor = 0.5
learn_rate = 0.05
epsilon = 1e-08
skew = 3
NT = (((1,), (1,)), ((), ()))


def flip(index, bit):
    return index + bit * (1 - 2 * ((index // bit) % 2))


def pieces_of(shard_rows, n_wide):
    pieces = 1
    while n_wide % (2 * pieces) == 0 and shard_rows % (32 * pieces) == 0:
        pieces *= 2
    return pieces


def masks_of(pieces):
    across = list(range(2, pieces, 2))
    return [masks for masks in (across, [1] if pieces > 1 else []) if masks]


def flips(index, mask):
    bit = 1
    while bit <= mask:
        if mask & bit:
            index = flip(index, bit)
        bit *= 2
    return index


def tower_kernel(
    n_wide, n_narrow, pieces, scale, limit,
    pooled_hbm, cot_hbm, w1_hbm, w2_hbm, bias_ref, counts_hbm, out_ref,
    pooled, cot, w1, w2, looks, hidden, back, deltas, gfull, gsend, grecv, sums,
    local_sem, wsend_sem, wrecv_sem, csend_sem, crecv_sem, gsend_sem, grecv_sem,
    asend_sem, arecv_sem,
):
    wide = lax.axis_index("wide")
    narrow = lax.axis_index("narrow")
    shard = w1_hbm.shape[0]
    piece_rows = shard // pieces
    bags = pooled.shape[0]
    inner = w1.shape[1]
    emb = gfull.shape[3]
    tables, slots = looks.shape[1], looks.shape[2]
    rest = n_narrow - 1
    part = wide % pieces
    base = wide - part
    masks = masks_of(pieces)
    half = inner // 2
    units = [
        (w1, w1_hbm, pl.ds(0, half)),
        (w1, w1_hbm, pl.ds(half, half)),
        (w2, w2_hbm, pl.ds(0, w2.shape[1])),
    ]
    stages = len(masks)

    def lane_block(index, size):
        return pl.ds(pl.multiple_of(index * size, size), size)

    def local(step, src, dst):
        return pltpu.make_async_copy(src, dst, local_sem.at[step])

    own_rows = lane_block(narrow, shard)
    locals_ = [
        local(0, pooled_hbm, pooled),
        local(1, w1_hbm, w1.at[own_rows, :]),
        local(2, cot_hbm, cot),
        local(3, w2_hbm, w2.at[own_rows, :]),
        local(4, counts_hbm.at[:, :, lane_block(narrow, bags)], looks.at[narrow]),
    ]
    for copy in locals_:
        copy.start()

    barrier = pltpu.get_barrier_semaphore()
    for d in range(1, n_narrow):
        pl.semaphore_signal(
            barrier, inc=1, device_id={"narrow": (narrow + d) % n_narrow}, device_id_type=MESH
        )
    for d in range(1, n_wide):
        pl.semaphore_signal(
            barrier, inc=1, device_id={"wide": (wide + d) % n_wide}, device_id_type=MESH
        )
    pl.semaphore_wait(barrier, n_narrow + n_wide - 2)

    def remote(src, dst, send, recv, device):
        return pltpu.make_async_remote_copy(
            src_ref=src, dst_ref=dst, send_sem=send, recv_sem=recv,
            device_id=device, device_id_type=MESH,
        )

    sent = []

    def launch(copy):
        copy.start()
        sent.append(copy)

    def rows_at(source, piece):
        return pl.ds(pl.multiple_of(source * shard + piece * piece_rows, piece_rows), piece_rows)

    for d in range(rest):
        target = {"narrow": (narrow + d + 1) % n_narrow}
        for u, (ref, shard_ref, columns) in enumerate(units):
            launch(remote(
                shard_ref.at[lane_block(part, piece_rows), columns],
                ref.at[rows_at(narrow, part), columns],
                wsend_sem.at[u, d, 0], wrecv_sem.at[u, d, 0], target,
            ))
    for d in range(rest):
        owner = (narrow + d + 1) % n_narrow
        launch(remote(
            counts_hbm.at[:, :, lane_block(owner, bags)], looks.at[narrow],
            csend_sem.at[d], crecv_sem.at[d], {"narrow": owner},
        ))

    held = [[[part] for _ in range(rest)] for _ in units]

    def stage_arrive(u, d, stage):
        source = (narrow + n_narrow - d - 1) % n_narrow
        ref, _, columns = units[u]
        if stage == 0:
            moves = [(part, {"narrow": source})]
            first = 0
        else:
            moves = [
                (flips(q, mask), {"wide": base + flips(part, mask)})
                for mask in masks[stage - 1] for q in held[u][d]
            ]
            first = len(held[u][d])
        for i, (q, device) in enumerate(moves):
            view = ref.at[rows_at(source, q), columns]
            remote(
                view, view, wsend_sem.at[u, d, first + i], wrecv_sem.at[u, d, first + i], device
            ).wait_recv()
        if stage:
            held[u][d] = held[u][d] + [q for q, _ in moves]

    def stage_send(u, d, stage):
        source = (narrow + n_narrow - d - 1) % n_narrow
        ref, _, columns = units[u]
        slot = len(held[u][d])
        for mask in masks[stage]:
            for q in held[u][d]:
                view = ref.at[rows_at(source, q), columns]
                launch(remote(
                    view, view, wsend_sem.at[u, d, slot], wrecv_sem.at[u, d, slot],
                    {"wide": base + flips(part, mask)},
                ))
                slot += 1

    tile = min(256, inner)

    def add_chunk(source, fresh):
        rows = lane_block(source, shard)
        lhs = pooled[:, rows]

        def body(t, carry):
            columns = lane_block(t, tile)
            value = jnp.dot(lhs, w1[rows, columns], preferred_element_type=jnp.float32)
            if fresh:
                hidden[:, columns] = value
            else:
                hidden[:, columns] = hidden[:, columns] + value
            return carry

        lax.fori_loop(0, inner // tile, body, 0)
        back[:, rows] = lax.dot_general(
            cot[...], w2[rows, :], NT, preferred_element_type=jnp.float32
        )

    chunked = shard % 128 == 0
    for copy in locals_:
        copy.wait()
    if chunked:
        add_chunk(narrow, True)
    items = rest * len(units)
    for t in range(items + skew * stages):
        for stage in range(stages + 1):
            item = t - skew * stage
            if 0 <= item < items:
                d, u = divmod(item, len(units))
                stage_arrive(u, d, stage)
                if stage < stages:
                    stage_send(u, d, stage)
                elif chunked and u == len(units) - 1:
                    add_chunk((narrow + n_narrow - d - 1) % n_narrow, False)

    def activate(t, carry):
        columns = lane_block(t, tile)
        if chunked:
            value = hidden[:, columns]
            back_value = back[:, columns]
        else:
            value = jnp.dot(pooled[...], w1[:, columns], preferred_element_type=jnp.float32)
            back_value = lax.dot_general(
                cot[...], w2[columns, :], NT, preferred_element_type=jnp.float32
            )
        value = value + bias_ref[:, columns]
        sig = jax.nn.sigmoid(value)
        slopes = sig * (1.0 + value * (1.0 - sig))
        deltas[:, columns] = (back_value * slopes).astype(jnp.bfloat16)
        return carry

    lax.fori_loop(0, inner // tile, activate, 0)

    for d in range(rest):
        source = (narrow + n_narrow - d - 1) % n_narrow
        view = looks.at[source]
        remote(view, view, csend_sem.at[d], crecv_sem.at[d], {"narrow": source}).wait_recv()

    groups = tables // 2
    for t in range(groups):
        wrows = w1[2 * t * emb:2 * (t + 1) * emb, :]
        grad_in = lax.dot_general(
            deltas[...], wrows, NT, preferred_element_type=jnp.float32
        ).astype(jnp.bfloat16)
        for i in range(2):
            k = 2 * t + i
            lookups = looks[:, k].reshape(n_narrow * slots, bags)
            value = jnp.dot(
                lookups, grad_in[:, i * emb:(i + 1) * emb], preferred_element_type=jnp.float32
            )
            for owner in range(n_narrow):
                rows = value[owner * slots:(owner + 1) * slots]
                gfull[owner, k] = rows
                gsend[owner, k] = rows.astype(jnp.bfloat16)
        block = pl.ds(2 * t, 2)
        for d in range(rest):
            owner = (narrow + d + 1) % n_narrow
            launch(remote(
                gsend.at[owner, block], grecv.at[narrow, block],
                gsend_sem.at[d, t], grecv_sem.at[d, t], {"narrow": owner},
            ))
    for t in range(groups):
        block = pl.ds(2 * t, 2)
        total = gfull[narrow, block]
        for d in range(rest):
            source = (narrow + n_narrow - d - 1) % n_narrow
            view = grecv.at[source, block]
            remote(view, view, gsend_sem.at[d, t], grecv_sem.at[d, t], {"narrow": source}).wait_recv()
            total = total + grecv[source, block].astype(jnp.float32)
        grads = total * scale
        norms = jnp.sqrt(jnp.sum(grads * grads, axis=-1, keepdims=True))
        sums[wide, block] = (grads * (limit / jnp.maximum(norms, limit))).astype(jnp.bfloat16)
        for e in range(n_wide - 1):
            launch(remote(
                sums.at[wide, block], sums.at[wide, block],
                asend_sem.at[t, e], arecv_sem.at[t, e], {"wide": (wide + e + 1) % n_wide},
            ))
    for t in range(groups):
        block = pl.ds(2 * t, 2)
        for e in range(n_wide - 1):
            source = (wide + n_wide - e - 1) % n_wide
            view = sums.at[source, block]
            remote(view, view, asend_sem.at[t, e], arecv_sem.at[t, e], {"wide": source}).wait_recv()
        summed = sums[0, block].astype(jnp.float32)
        for q in range(1, n_wide):
            summed = summed + sums[q, block].astype(jnp.float32)
        out_ref[block] = summed
    for copy in sent:
        copy.wait_send()


def update_kernel(ids_ref, summed_ref, table_ref, accum_ref, new_table_ref, new_accum_ref):
    tables, slots = ids_ref.shape
    new_table_ref[...] = table_ref[...]
    new_accum_ref[...] = accum_ref[...]
    for k in range(tables):
        for a in range(slots):
            row = pl.ds(ids_ref[k, a], 1)
            value = summed_ref[k, a:a + 1, :]
            grown = accum_ref[k, row, :] + value * value
            new_accum_ref[k, row, :] = grown
            new_table_ref[k, row, :] = table_ref[k, row, :] - learn_rate * value / (
                jnp.sqrt(grown) + epsilon
            )


def shards(n_wide, n_narrow, pooled, cotangent, w_first, b_first, w_second, counts, row_ids, table, accum):
    tables, slots, group_bags = counts.shape
    emb = table.shape[2]
    bags, emb_all = pooled.shape
    shard, inner = w_first.shape
    top = w_second.shape[1]
    pieces = pieces_of(shard, n_wide)
    rest = n_narrow - 1
    groups = tables // 2
    scale = 1.0 / math.sqrt(group_bags)
    limit = clip_factor * math.sqrt(emb)
    hbm = pl.BlockSpec(memory_space=pl.ANY)
    vmem = pl.BlockSpec(memory_space=pltpu.VMEM)
    dma = pltpu.SemaphoreType.DMA
    summed = pl.pallas_call(
        functools.partial(tower_kernel, n_wide, n_narrow, pieces, scale, limit),
        out_shape=jax.ShapeDtypeStruct((tables, slots, emb), jnp.float32),
        in_specs=[hbm, hbm, hbm, hbm, vmem, hbm],
        out_specs=vmem,
        scratch_shapes=[
            pltpu.VMEM((bags, emb_all), jnp.bfloat16),
            pltpu.VMEM((bags, top), jnp.bfloat16),
            pltpu.VMEM((emb_all, inner), jnp.bfloat16),
            pltpu.VMEM((inner, top), jnp.bfloat16),
            pltpu.VMEM((n_narrow, tables, slots, bags), jnp.bfloat16),
            pltpu.VMEM((bags, inner), jnp.float32),
            pltpu.VMEM((bags, inner), jnp.float32),
            pltpu.VMEM((bags, inner), jnp.bfloat16),
            pltpu.VMEM((n_narrow, tables, slots, emb), jnp.float32),
            pltpu.VMEM((n_narrow, tables, slots, emb), jnp.bfloat16),
            pltpu.VMEM((n_narrow, tables, slots, emb), jnp.bfloat16),
            pltpu.VMEM((n_wide, tables, slots, emb), jnp.bfloat16),
            dma((5,)),
            dma((3, rest, pieces)),
            dma((3, rest, pieces)),
            dma((rest,)),
            dma((rest,)),
            dma((rest, groups)),
            dma((rest, groups)),
            dma((groups, n_wide - 1)),
            dma((groups, n_wide - 1)),
        ],
        compiler_params=pltpu.CompilerParams(
            collective_id=0, has_side_effects=True, vmem_limit_bytes=56 * 1024 * 1024
        ),
        name="tower",
    )(pooled, cotangent, w_first, w_second, b_first.reshape(1, inner), counts)
    return pl.pallas_call(
        update_kernel,
        out_shape=(
            jax.ShapeDtypeStruct(table.shape, table.dtype),
            jax.ShapeDtypeStruct(accum.shape, accum.dtype),
        ),
        in_specs=[pl.BlockSpec(memory_space=pltpu.SMEM), vmem, vmem, vmem],
        out_specs=(vmem, vmem),
        name="update",
    )(row_ids, summed, table, accum)


def solution(mesh):
    in_specs = (
        P(("wide", "narrow"), None),
        P(("wide", "narrow"), None),
        P("narrow", None),
        P(),
        P("narrow", None),
        P(None, "narrow", "wide"),
        P(None, "narrow"),
        P(None, "narrow", None),
        P(None, "narrow", None),
    )
    out_specs = (P(None, "narrow", None), P(None, "narrow", None))
    step = functools.partial(shards, mesh.shape["wide"], mesh.shape["narrow"])
    return jax.shard_map(step, mesh=mesh, in_specs=in_specs, out_specs=out_specs, check_vma=False)
```

profile of v0, /device:TPU:0, one launch (start us, length us, event | category | flops | bytes accessed | tf_op | source)
XLA Modules:
  0.0 45.0 jit_solution(8373791798289210982)
XLA Ops:
  0.6 42.2 %tower.1.summed_ref = f32[8,16,128]{2,1,0:T(8,128)} custom-call(bf16[512,1024]{1,0:T(8,128)(2,1)} %pooled_hbm.1, bf16[512,512]{1,0:T(8,128)(2,1)} %cot_hbm.1, bf16[256,1024]{1,0:T(8,128)(2,1)} %w1_hbm.1, bf16[256,512]{1,0:T(8,128)(2,1)} %w2_hbm.1, f32[1,1024]{1,0:T(1,128)} %bitcast.1, bf16[8,16,2048]{2,1,0:T(8,128)(2,1)} %counts_hbm.1), custom_call_target="tpu_custom_call" | custom-call | tf_op jit(solution)/shard_map/tower/pallas_call | solution.py:306
  42.8 2.1 %update.1 = (f32[8,64,128]{2,1,0:T(8,128)}, f32[8,64,128]{2,1,0:T(8,128)}) custom-call(s32[8,16]{1,0:T(8,128)} %ids_ref.1, f32[8,16,128]{2,1,0:T(8,128)} %tower.1.summed_ref, f32[8,64,128]{2,1,0:T(8,128)} %table_ref.1, f32[8,64,128]{2,1,0:T(8,128)} %accum_ref.1), custom_call_target="tpu_custom_call" | custom-call | tf_op jit(solution)/shard_map/update/pallas_call | solution.py:339
where the time goes:
time: 45.1 us; the launch traced here: 45 us
  Pallas kernels  44.3 us (98%)
  between operations  0.64 us (1%)
    pallas_call x1, Pallas kernels, shards(): pl.pallas_call(functools.partial(tower_kernel, n_wide, n_narrow, pieces,...  42.2 us
    pallas_call x1, Pallas kernels, shards(): pl.pallas_call(update_kernel, out_shape=(jax.ShapeDtypeStruct(table.shape...  2.14 us

commit v1 on v0

--- a/solution.py
+++ b/solution.py
@@ -43,10 +43,9 @@
 
 def tower_kernel(
     n_wide, n_narrow, pieces, scale, limit,
-    pooled_hbm, cot_hbm, w1_hbm, w2_hbm, bias_ref, counts_hbm, out_ref,
+    pooled_hbm, cot_hbm, w1_hbm, w2_hbm, bias_ref, counts_hbm, ids_ref, out_ref,
     pooled, cot, w1, w2, looks, hidden, back, deltas, gfull, gsend, grecv, sums,
-    local_sem, wsend_sem, wrecv_sem, csend_sem, crecv_sem, gsend_sem, grecv_sem,
-    asend_sem, arecv_sem,
+    local_sem, send_sem, wrecv_sem, crecv_sem, grecv_sem, arecv_sem,
 ):
     wide = lax.axis_index("wide")
     narrow = lax.axis_index("narrow")
@@ -117,13 +116,13 @@
             launch(remote(
                 shard_ref.at[lane_block(part, piece_rows), columns],
                 ref.at[rows_at(narrow, part), columns],
-                wsend_sem.at[u, d, 0], wrecv_sem.at[u, d, 0], target,
+                send_sem, wrecv_sem.at[u, d, 0], target,
             ))
     for d in range(rest):
         owner = (narrow + d + 1) % n_narrow
         launch(remote(
             counts_hbm.at[:, :, lane_block(owner, bags)], looks.at[narrow],
-            csend_sem.at[d], crecv_sem.at[d], {"narrow": owner},
+            send_sem, crecv_sem.at[d], {"narrow": owner},
         ))
 
     held = [[[part] for _ in range(rest)] for _ in units]
@@ -143,7 +142,7 @@
         for i, (q, device) in enumerate(moves):
             view = ref.at[rows_at(source, q), columns]
             remote(
-                view, view, wsend_sem.at[u, d, first + i], wrecv_sem.at[u, d, first + i], device
+                view, view, send_sem, wrecv_sem.at[u, d, first + i], device
             ).wait_recv()
         if stage:
             held[u][d] = held[u][d] + [q for q, _ in moves]
@@ -156,7 +155,7 @@
             for q in held[u][d]:
                 view = ref.at[rows_at(source, q), columns]
                 launch(remote(
-                    view, view, wsend_sem.at[u, d, slot], wrecv_sem.at[u, d, slot],
+                    view, view, send_sem, wrecv_sem.at[u, d, slot],
                     {"wide": base + flips(part, mask)},
                 ))
                 slot += 1
@@ -167,16 +166,11 @@
         rows = lane_block(source, shard)
         lhs = pooled[:, rows]
 
-        def body(t, carry):
-            columns = lane_block(t, tile)
-            value = jnp.dot(lhs, w1[rows, columns], preferred_element_type=jnp.float32)
-            if fresh:
-                hidden[:, columns] = value
-            else:
-                hidden[:, columns] = hidden[:, columns] + value
-            return carry
-
-        lax.fori_loop(0, inner // tile, body, 0)
+        value = jnp.dot(lhs, w1[rows, :], preferred_element_type=jnp.float32)
+        if fresh:
+            hidden[...] = value
+        else:
+            hidden[...] = hidden[...] + value
         back[:, rows] = lax.dot_general(
             cot[...], w2[rows, :], NT, preferred_element_type=jnp.float32
         )
@@ -219,7 +213,7 @@
     for d in range(rest):
         source = (narrow + n_narrow - d - 1) % n_narrow
         view = looks.at[source]
-        remote(view, view, csend_sem.at[d], crecv_sem.at[d], {"narrow": source}).wait_recv()
+        remote(view, view, send_sem, crecv_sem.at[d], {"narrow": source}).wait_recv()
 
     groups = tables // 2
     for t in range(groups):
@@ -242,7 +236,7 @@
             owner = (narrow + d + 1) % n_narrow
             launch(remote(
                 gsend.at[owner, block], grecv.at[narrow, block],
-                gsend_sem.at[d, t], grecv_sem.at[d, t], {"narrow": owner},
+                send_sem, grecv_sem.at[d, t], {"narrow": owner},
             ))
     for t in range(groups):
         block = pl.ds(2 * t, 2)
@@ -250,7 +244,7 @@
         for d in range(rest):
             source = (narrow + n_narrow - d - 1) % n_narrow
             view = grecv.at[source, block]
-            remote(view, view, gsend_sem.at[d, t], grecv_sem.at[d, t], {"narrow": source}).wait_recv()
+            remote(view, view, send_sem, grecv_sem.at[d, t], {"narrow": source}).wait_recv()
             total = total + grecv[source, block].astype(jnp.float32)
         grads = total * scale
         norms = jnp.sqrt(jnp.sum(grads * grads, axis=-1, keepdims=True))
@@ -258,35 +252,26 @@
         for e in range(n_wide - 1):
             launch(remote(
                 sums.at[wide, block], sums.at[wide, block],
-                asend_sem.at[t, e], arecv_sem.at[t, e], {"wide": (wide + e + 1) % n_wide},
+                send_sem, arecv_sem.at[t, e], {"wide": (wide + e + 1) % n_wide},
             ))
     for t in range(groups):
         block = pl.ds(2 * t, 2)
         for e in range(n_wide - 1):
             source = (wide + n_wide - e - 1) % n_wide
             view = sums.at[source, block]
-            remote(view, view, asend_sem.at[t, e], arecv_sem.at[t, e], {"wide": source}).wait_recv()
+            remote(view, view, send_sem, arecv_sem.at[t, e], {"wide": source}).wait_recv()
         summed = sums[0, block].astype(jnp.float32)
         for q in range(1, n_wide):
             summed = summed + sums[q, block].astype(jnp.float32)
-        out_ref[block] = summed
+        for i in range(2):
+            k = 2 * t + i
+            hot = lax.broadcasted_iota(jnp.int32, (out_ref.shape[1], slots), 0) == ids_ref[k:k + 1, :]
+            out_ref[k] = jnp.dot(
+                hot.astype(jnp.float32), summed[i], precision=lax.Precision.HIGHEST,
+                preferred_element_type=jnp.float32,
+            )
     for copy in sent:
         copy.wait_send()
-
-
-def update_kernel(ids_ref, summed_ref, table_ref, accum_ref, new_table_ref, new_accum_ref):
-    tables, slots = ids_ref.shape
-    new_table_ref[...] = table_ref[...]
-    new_accum_ref[...] = accum_ref[...]
-    for k in range(tables):
-        for a in range(slots):
-            row = pl.ds(ids_ref[k, a], 1)
-            value = summed_ref[k, a:a + 1, :]
-            grown = accum_ref[k, row, :] + value * value
-            new_accum_ref[k, row, :] = grown
-            new_table_ref[k, row, :] = table_ref[k, row, :] - learn_rate * value / (
-                jnp.sqrt(grown) + epsilon
-            )
 
 
 def shards(n_wide, n_narrow, pooled, cotangent, w_first, b_first, w_second, counts, row_ids, table, accum):
@@ -305,8 +290,8 @@
     dma = pltpu.SemaphoreType.DMA
     summed = pl.pallas_call(
         functools.partial(tower_kernel, n_wide, n_narrow, pieces, scale, limit),
-        out_shape=jax.ShapeDtypeStruct((tables, slots, emb), jnp.float32),
-        in_specs=[hbm, hbm, hbm, hbm, vmem, hbm],
+        out_shape=jax.ShapeDtypeStruct(table.shape, jnp.float32),
+        in_specs=[hbm, hbm, hbm, hbm, vmem, hbm, vmem],
         out_specs=vmem,
         scratch_shapes=[
             pltpu.VMEM((bags, emb_all), jnp.bfloat16),
@@ -322,30 +307,19 @@
             pltpu.VMEM((n_narrow, tables, slots, emb), jnp.bfloat16),
             pltpu.VMEM((n_wide, tables, slots, emb), jnp.bfloat16),
             dma((5,)),
-            dma((3, rest, pieces)),
+            dma,
             dma((3, rest, pieces)),
             dma((rest,)),
-            dma((rest,)),
             dma((rest, groups)),
-            dma((rest, groups)),
-            dma((groups, n_wide - 1)),
             dma((groups, n_wide - 1)),
         ],
         compiler_params=pltpu.CompilerParams(
             collective_id=0, has_side_effects=True, vmem_limit_bytes=56 * 1024 * 1024
         ),
         name="tower",
-    )(pooled, cotangent, w_first, w_second, b_first.reshape(1, inner), counts)
-    return pl.pallas_call(
-        update_kernel,
-        out_shape=(
-            jax.ShapeDtypeStruct(table.shape, table.dtype),
-            jax.ShapeDtypeStruct(accum.shape, accum.dtype),
-        ),
-        in_specs=[pl.BlockSpec(memory_space=pltpu.SMEM), vmem, vmem, vmem],
-        out_specs=(vmem, vmem),
-        name="update",
-    )(row_ids, summed, table, accum)
+    )(pooled, cotangent, w_first, w_second, b_first.reshape(1, inner), counts, row_ids)
+    new_accum = accum + summed * summed
+    return table - learn_rate * summed / (jnp.sqrt(new_accum) + epsilon), new_accum
 
 
 def solution(mesh):

time: 45.1 us -> 43.1 us (0.956)
  Pallas kernels: 44.3 us -> 40.4 us
  other arithmetic: 0 us -> 1.85 us
    pallas_call x1 -> x0, Pallas kernels: 2.14 us -> none  [shards(): pl.pallas_call(update_kernel, out_shape=(jax.ShapeDtypeStruct(table.shape...]
    sub x0 -> x1, other arithmetic: none -> 1.85 us  [shards(): table - learn_rate * summed / (jnp.sqrt(new_accum) + epsilon)]
    pallas_call x1, Pallas kernels: 42.2 us -> 40.4 us  [shards(): pl.pallas_call(functools.partial(tower_kernel, n_wide, n_narrow, pieces,...]
where the time goes in v1:
time: 43.1 us; the launch traced here: 42.9 us
  Pallas kernels  40.4 us (94%)
  other arithmetic  1.85 us (4%)
  between operations  0.67 us (2%)
    pallas_call x1, Pallas kernels, shards(): pl.pallas_call(functools.partial(tower_kernel, n_wide, n_narrow, pieces,...  40.4 us
    sub x1, other arithmetic, shards(): table - learn_rate * summed / (jnp.sqrt(new_accum) + epsilon)  1.85 us

profile of v1, /device:TPU:0, one launch (start us, length us, event | category | flops | bytes accessed | tf_op | source)
XLA Modules:
  0.0 42.9 jit_solution(3462947944619175269)
XLA Ops:
  0.6 0.0 copy-start
  0.6 0.0 copy-start.1
  0.7 40.4 %tower.1 = f32[8,64,128]{2,1,0:T(8,128)} custom-call(bf16[512,1024]{1,0:T(8,128)(2,1)} %pooled_hbm.1, bf16[512,512]{1,0:T(8,128)(2,1)} %cot_hbm.1, bf16[256,1024]{1,0:T(8,128)(2,1)} %w1_hbm.1, bf16[256,512]{1,0:T(8,128)(2,1)} %w2_hbm.1, f32[1,1024]{1,0:T(1,128)} %bitcast.1, bf16[8,16,2048]{2,1,0:T(8,128)(2,1)} %counts_hbm.1, s32[8,16]{1,0:T(8,128)} %ids_ref.1), custom_call_target="tpu_custom_call" | custom-call | tf_op jit(solution)/shard_map/tower/pallas_call | solution.py:291
  41.1 0.0 copy-done
  41.1 0.0 copy-done.1
  41.1 1.9 %divide_subtract_fusion = (f32[8,64,128]{2,1,0:T(8,128)}, f32[8,64,128]{2,1,0:T(8,128)}) fusion(f32[8,64,128]{2,1,0:T(8,128)S(1)} %copy-done, f32[8,64,128]{2,1,0:T(8,128)} %tower.1, f32[8,64,128]{2,1,0:T(8,128)S(1)} %copy-done.1), kind=kLoop, calls=%fused_computation | loop fusion | flops 393216 | bytes 1310720 | tf_op jit(solution)/shard_map/sub | solution.py:322
Async XLA Ops:
  0.6 40.4 %copy-start = (f32[8,64,128]{2,1,0:T(8,128)S(1)}, f32[8,64,128]{2,1,0:T(8,128)}, u32[]{:S(2)}) copy-start(f32[8,64,128]{2,1,0:T(8,128)} %param.16) | copy-start | bytes 786436
  0.6 40.4 %copy-start.1 = (f32[8,64,128]{2,1,0:T(8,128)S(1)}, f32[8,64,128]{2,1,0:T(8,128)}, u32[]{:S(2)}) copy-start(f32[8,64,128]{2,1,0:T(8,128)} %param.17) | copy-start | bytes 786436

commit v2 on v1

v2 whole, which is shorter than its diff:
```python
import functools
import math

import jax
import jax.numpy as jnp
from jax import lax
from jax.experimental import pallas as pl
from jax.experimental.pallas import tpu as pltpu
from jax.sharding import PartitionSpec as P

MESH = pl.DeviceIdType.MESH
clip_factor = 0.5
learn_rate = 0.05
epsilon = 1e-08
NT = (((1,), (1,)), ((), ()))
ROUTES = ("xy", "yx", "hw")
DEFER = 8
LAG_SIDE = 6
LAG_DIAG = 10
VMEM_KIB = 32 * 1024


def flip(index, mask):
    bit = 1
    while bit <= mask:
        if mask & bit:
            index = index + bit * (1 - 2 * ((index // bit) % 2))
        bit *= 2
    return index


def pieces_of(shard_rows, n_wide):
    pieces = 1
    while pieces < 8 and n_wide % (2 * pieces) == 0 and shard_rows % (32 * pieces) == 0:
        pieces *= 2
    return pieces


def arrivals(n, n_narrow, count):
    items = []
    for s in range(n_narrow):
        if s != n:
            for v in range(count):
                items.append(((abs(s - n) - 1) * count + v, s > n, s, v))
    return [(s, v) for _, _, s, v in sorted(items)]


def tower_kernel(
    n_wide, n_narrow, pieces, scale, limit,
    pooled_hbm, cot_hbm, w1_hbm, w2_hbm, bias_hbm, counts_hbm, ids_hbm, out_ref,
    pooled, cot, weights, bias, ids, looks, hidden, back, deltas, grad_in, gfull, gsend, grecv, sums,
    local_sem, send_sem, z_sem, x_sem, y_sem, d_sem, c_sem, look_sem, grad_sem, sum_sem,
):
    wide = lax.axis_index("wide")
    narrow = lax.axis_index("narrow")
    shard, inner = w1_hbm.shape
    top = w2_hbm.shape[1]
    units = inner // top + 1
    piece_rows = shard // pieces
    bags = pooled.shape[0]
    emb = gfull.shape[3]
    tables, slots = looks.shape[1], looks.shape[2]
    rest = n_narrow - 1
    part = wide % pieces
    base = wide - part
    has_core, has_x, has_y = pieces >= 2, pieces >= 4, pieces >= 8
    routes = [ROUTES[u % len(ROUTES)] for u in range(units)] if has_y else ["none"] * units
    chained = [u for u in range(units) if routes[u] == "z"]
    per_source = units + len(chained)

    def lane_block(index, size):
        return pl.ds(pl.multiple_of(index * size, size), size)

    def local(step, src, dst):
        return pltpu.make_async_copy(src, dst, local_sem.at[step])

    own_rows = lane_block(narrow, shard)
    own_w = [
        local(0, w1_hbm, weights.at[own_rows, pl.ds(0, inner)]),
        local(1, w2_hbm, weights.at[own_rows, pl.ds(inner, top)]),
    ]
    own_x = [local(2, pooled_hbm, pooled), local(3, cot_hbm, cot)]
    own_rest = [
        local(4, counts_hbm.at[:, :, lane_block(narrow, bags)], looks.at[narrow]),
        local(5, bias_hbm, bias),
        local(6, ids_hbm, ids),
    ]
    for copy in own_w + own_x + own_rest:
        copy.start()

    barrier = pltpu.get_barrier_semaphore()

    def greet(device):
        pl.semaphore_signal(barrier, inc=1, device_id=device, device_id_type=MESH)

    @pl.when(narrow > 0)
    def _():
        greet({"narrow": narrow - 1})

    @pl.when(narrow < n_narrow - 1)
    def _():
        greet({"narrow": narrow + 1})

    if pieces == n_wide:
        beside = [base + flip(part, m) for m in (1, 2, 4) if m < pieces]
    else:
        beside = [(wide + d) % n_wide for d in range(1, n_wide)]
    for device in beside:
        greet({"wide": device})
    ends = jnp.where(narrow > 0, 1, 0) + jnp.where(narrow < n_narrow - 1, 1, 0)
    pl.semaphore_wait(barrier, ends + len(beside))

    def remote(src, dst, recv, device):
        return pltpu.make_async_remote_copy(
            src_ref=src, dst_ref=dst, send_sem=send_sem, recv_sem=recv,
            device_id=device, device_id_type=MESH,
        )

    sent = []

    def launch(copy, cond=None):
        if cond is None:
            copy.start()
        else:
            @pl.when(cond)
            def _():
                copy.start()
        sent.append((copy, cond))

    def pick(values):
        if all(v == values[0] for v in values):
            return values[0]
        total = 0
        for n, v in enumerate(values):
            total = total + jnp.where(narrow == n, v, 0)
        return total

    def slot_of(s, n):
        return (s - n + n_narrow) % n_narrow - 1

    def view(s, q, u):
        rows = pl.ds(pl.multiple_of(s * shard + q * piece_rows, piece_rows), piece_rows)
        return weights.at[rows, lane_block(u, top)]

    def any_of(u, chosen):
        hit = u == chosen[0]
        for c in chosen[1:]:
            hit = jnp.logical_or(hit, u == c)
        return hit

    def on_route(s, u, route):
        if route == "hw":
            return False
        return (u + jnp.where(u == units - 1, s, 0)) % 2 == (0 if route == "xy" else 1)

    for copy in own_w:
        copy.wait()
    for v in range(per_source):
        u = v if v < units else chained[v - units]
        q = part if v < units else flip(part, 6)
        w = view(narrow, q, u)
        for ahead, cond in ((narrow + 1, narrow < n_narrow - 1), (narrow - 1, narrow > 0)):
            launch(remote(w, w, z_sem.at[slot_of(narrow, ahead), v], {"narrow": ahead}), cond)

    order = [arrivals(n, n_narrow, per_source) for n in range(n_narrow)]
    side = [[(s, v) for s, v in order[n] if v < units] for n in range(n_narrow)]
    diag = [[(s, v) for s, v in side[n] if routes[v] != "z"] for n in range(n_narrow)]
    n_z = len(order[0])
    side_at = [order[0].index(item) + LAG_SIDE for item in side[0]]
    diag_at = [order[0].index(item) + LAG_DIAG for item in diag[0]]
    if not has_x:
        side_at = []
    if not has_y:
        diag_at = []

    def to_core(w, slot):
        if has_core:
            launch(remote(w, w, c_sem.at[slot], {"wide": base + flip(part, 1)}))

    def await_view(w, sem):
        remote(w, w, sem, {"wide": base + flip(part, 1)} if has_core else {"narrow": narrow}).wait_recv()

    def z_event(t):
        s, v = pick([o[t][0] for o in order]), pick([o[t][1] for o in order])
        slot = slot_of(s, narrow)
        u, q, mine = v, part, None
        if chained:
            mine = v < units
            extra = 0
            for i, c in enumerate(chained):
                extra = extra + jnp.where(v == units + i, c, 0)
            u = jnp.where(mine, v, extra)
            q = jnp.where(mine, part, flip(part, 6))
        w = view(s, q, u)
        await_view(w, z_sem.at[slot, v])
        ahead = jnp.where(s < narrow, narrow + 1, narrow - 1)
        inside = jnp.logical_and(ahead >= 0, ahead < n_narrow)
        launch(remote(w, w, z_sem.at[slot_of(s, ahead), v], {"narrow": ahead}), inside)
        if has_x:
            launch(remote(w, w, x_sem.at[slot, u], {"wide": base + flip(part, 2)}), mine)
        if has_y:
            launch(remote(w, w, y_sem.at[slot, u], {"wide": base + flip(part, 4)}), mine)
            direct = on_route(s, u, "hw")
            if direct is not False:
                if mine is not None:
                    direct = jnp.logical_and(direct, mine)
                launch(remote(w, w, d_sem.at[slot, u], {"wide": base + flip(part, 6)}), direct)
        to_core(w, slot)

    def side_event(j):
        s, u = pick([o[j][0] for o in side]), pick([o[j][1] for o in side])
        slot = slot_of(s, narrow)
        for name, mask, sem, there, route in (
            ("x", 2, x_sem, 4, "xy"), ("y", 4, y_sem, 2, "yx"),
        ):
            if mask < pieces:
                w = view(s, flip(part, mask), u)
                await_view(w, sem.at[slot, u])
                onward = on_route(s, u, route)
                if onward is not False:
                    launch(remote(w, w, d_sem.at[slot, u], {"wide": base + flip(part, there)}), onward)
                to_core(w, slot)

    def diag_event(j):
        s, u = pick([o[j][0] for o in diag]), pick([o[j][1] for o in diag])
        slot = slot_of(s, narrow)
        w = view(s, flip(part, 6), u)
        await_view(w, d_sem.at[slot, u])
        to_core(w, slot)

    def add_chunk(source, fresh):
        rows = lane_block(source, shard)
        value = jnp.dot(
            pooled[:, rows], weights[rows, pl.ds(0, inner)], preferred_element_type=jnp.float32
        )
        if fresh:
            hidden[...] = value
        else:
            hidden[...] = hidden[...] + value
        back[:, rows] = lax.dot_general(
            cot[...], weights[rows, pl.ds(inner, top)], NT, preferred_element_type=jnp.float32
        )

    groups = tables // 2
    dests = []
    for n in range(n_narrow):
        plan = []
        for owner in range(n_narrow):
            if owner == n:
                continue
            seen = -1 if abs(owner - n) == 1 else order[n].index((owner, 0))
            relays = [t for t, (s, v) in enumerate(order[n]) if (s < n) == (owner > n)]
            plan.append((DEFER, abs(owner - n), owner))
        dests.append(sorted(plan))

    def send_looks(t):
        most = max(len([p for p in dests[n] if p[0] == t]) for n in range(n_narrow))
        if not most:
            return
        chosen = []
        for i in range(most):
            rows = [[p[2] for p in dests[n] if p[0] == t] for n in range(n_narrow)]
            owner = pick([r[i] if i < len(r) else (n + 1) % n_narrow for n, r in enumerate(rows)])
            valid = pick([1 if i < len(r) else 0 for r in rows])
            chosen.append((owner, valid))
        for g in range(groups):
            block = pl.ds(2 * g, 2)
            for owner, valid in chosen:
                launch(
                    remote(
                        counts_hbm.at[block, :, lane_block(owner, bags)], looks.at[narrow, block],
                        look_sem.at[g], {"narrow": owner},
                    ),
                    None if isinstance(valid, int) else valid == 1,
                )

    send_looks(-1)
    chunked = shard % 128 == 0
    for copy in own_x:
        copy.wait()
    if chunked:
        add_chunk(narrow, True)

    ranks = []
    for n in range(n_narrow):
        done = {}
        for t, (s, v) in enumerate(order[n]):
            done[s] = max(done.get(s, 0), t)
        for at, items in ((side_at, side[n]), (diag_at, diag[n])):
            for t, (s, v) in zip(at, items):
                done[s] = max(done[s], t)
        ranks.append(sorted((t, s) for s, t in done.items()))
    steps = max([n_z] + [t + 1 for t in side_at + diag_at])
    ready = [steps - 1] * rest
    for t in range(steps):
        if t < n_z:
            z_event(t)
        send_looks(t)
        if t in side_at:
            side_event(side_at.index(t))
        if t in diag_at:
            diag_event(diag_at.index(t))
        for i in range(rest):
            if ready[i] == t:
                s = pick([r[i][1] for r in ranks])
                if has_core:
                    w = weights.at[pl.ds(0, shard // 2), :]
                    await_view(w, c_sem.at[slot_of(s, narrow)])
                if chunked:
                    add_chunk(s, False)

    for copy in own_rest:
        copy.wait()
    if not chunked:
        hidden[...] = jnp.dot(
            pooled[...], weights[:, pl.ds(0, inner)], preferred_element_type=jnp.float32
        )
        back[...] = lax.dot_general(
            cot[...], weights[:, pl.ds(inner, top)], NT, preferred_element_type=jnp.float32
        )
    tile = min(256, inner)

    def activate(t, carry):
        columns = lane_block(t, tile)
        value = hidden[:, columns] + bias[:, columns]
        sig = jax.nn.sigmoid(value)
        slopes = sig * (1.0 + value * (1.0 - sig))
        deltas[:, columns] = (back[:, columns] * slopes).astype(jnp.bfloat16)
        return carry

    lax.fori_loop(0, inner // tile, activate, 0)

    far = [[s for _, s in sorted((-abs(s - n), s) for s in range(n_narrow) if s != n)] for n in range(n_narrow)]
    grad_in[...] = lax.dot_general(
        deltas[...], weights[:, pl.ds(0, inner)], NT, preferred_element_type=jnp.float32
    ).astype(jnp.bfloat16)
    for g in range(groups):
        await_view(looks.at[pl.ds(0, rest), pl.ds(2 * g, 2)], look_sem.at[g])
    for g in range(groups):
        lookups = looks[:, 2 * g:2 * (g + 1)].reshape(n_narrow * 2 * slots, bags)
        value = jnp.dot(
            lookups, grad_in[:, 2 * g * emb:2 * (g + 1) * emb], preferred_element_type=jnp.float32
        )
        value = value.reshape(n_narrow, 2, slots, 2 * emb)
        for i in range(2):
            rows = value[:, i, :, i * emb:(i + 1) * emb]
            gfull[:, 2 * g + i] = rows
            gsend[:, 2 * g + i] = rows.astype(jnp.bfloat16)
    for g in range(groups):
        block = pl.ds(2 * g, 2)
        for i in range(rest):
            owner = pick([f[i] for f in far])
            launch(remote(
                gsend.at[owner, block], grecv.at[slot_of(narrow, owner), block],
                grad_sem.at[g], {"narrow": owner},
            ))
    for g in range(groups):
        block = pl.ds(2 * g, 2)
        await_view(grecv.at[:, block], grad_sem.at[g])
        total = gfull[narrow, block]
        for d in range(rest):
            total = total + grecv[d, block].astype(jnp.float32)
        grads = total * scale
        norms = jnp.sqrt(jnp.sum(grads * grads, axis=-1, keepdims=True))
        sums[wide, block] = (grads * (limit / jnp.maximum(norms, limit))).astype(jnp.bfloat16)
        for e in range(n_wide - 1, 0, -1):
            peer = base + flip(part, e) if pieces == n_wide else (wide + e) % n_wide
            launch(remote(
                sums.at[wide, block], sums.at[wide, block], sum_sem.at[g], {"wide": peer},
            ))
    for g in range(groups):
        block = pl.ds(2 * g, 2)
        await_view(sums.at[pl.ds(0, n_wide - 1), block], sum_sem.at[g])
        summed = sums[0, block].astype(jnp.float32)
        for q in range(1, n_wide):
            summed = summed + sums[q, block].astype(jnp.float32)
        for i in range(2):
            k = 2 * g + i
            hot = lax.broadcasted_iota(jnp.int32, (out_ref.shape[1], slots), 0) == ids[k:k + 1, :]
            out_ref[k] = jnp.dot(
                hot.astype(jnp.float32), summed[i], precision=lax.Precision.HIGHEST,
                preferred_element_type=jnp.float32,
            )
    for copy, cond in sent:
        if cond is None:
            copy.wait_send()
        else:
            @pl.when(cond)
            def _():
                copy.wait_send()


def shards(n_wide, n_narrow, pooled, cotangent, w_first, b_first, w_second, counts, row_ids, table, accum):
    tables, slots, group_bags = counts.shape
    emb = table.shape[2]
    bags, emb_all = pooled.shape
    shard, inner = w_first.shape
    top = w_second.shape[1]
    units = inner // top + 1
    pieces = pieces_of(shard, n_wide)
    rest = n_narrow - 1
    groups = tables // 2
    scale = 1.0 / math.sqrt(group_bags)
    limit = clip_factor * math.sqrt(emb)
    hbm = pl.BlockSpec(memory_space=pl.ANY)
    vmem = pl.BlockSpec(memory_space=pltpu.VMEM)
    dma = pltpu.SemaphoreType.DMA
    summed = pl.pallas_call(
        functools.partial(tower_kernel, n_wide, n_narrow, pieces, scale, limit),
        out_shape=jax.ShapeDtypeStruct(table.shape, jnp.float32),
        in_specs=[hbm] * 7,
        out_specs=vmem,
        scratch_shapes=[
            pltpu.VMEM((bags, emb_all), jnp.bfloat16),
            pltpu.VMEM((bags, top), jnp.bfloat16),
            pltpu.VMEM((emb_all, inner + top), jnp.bfloat16),
            pltpu.VMEM((1, inner), jnp.float32),
            pltpu.VMEM(row_ids.shape, jnp.int32),
            pltpu.VMEM((n_narrow, tables, slots, bags), jnp.bfloat16),
            pltpu.VMEM((bags, inner), jnp.float32),
            pltpu.VMEM((bags, inner), jnp.float32),
            pltpu.VMEM((bags, inner), jnp.bfloat16),
            pltpu.VMEM((bags, emb_all), jnp.bfloat16),
            pltpu.VMEM((n_narrow, tables, slots, emb), jnp.float32),
            pltpu.VMEM((n_narrow, tables, slots, emb), jnp.bfloat16),
            pltpu.VMEM((rest, tables, slots, emb), jnp.bfloat16),
            pltpu.VMEM((n_wide, tables, slots, emb), jnp.bfloat16),
            dma((7,)),
            dma,
            dma((rest, units + len([r for r in ROUTES if r == "z"]))),
            dma((rest, units)),
            dma((rest, units)),
            dma((rest, units)),
            dma((rest,)),
            dma((groups,)),
            dma((groups,)),
            dma((groups,)),
        ],
        compiler_params=pltpu.CompilerParams(
            collective_id=0, has_side_effects=True, vmem_limit_bytes=VMEM_KIB * 1024
        ),
        name="tower",
    )(*[
        pltpu.with_memory_space_constraint(x, pltpu.HBM)
        for x in (pooled, cotangent, w_first, w_second, b_first.reshape(1, inner), counts, row_ids)
    ])
    new_accum = accum + summed * summed
    return table - learn_rate * summed / (jnp.sqrt(new_accum) + epsilon), new_accum


def solution(mesh):
    in_specs = (
        P(("wide", "narrow"), None),
        P(("wide", "narrow"), None),
        P("narrow", None),
        P(),
        P("narrow", None),
        P(None, "narrow", "wide"),
        P(None, "narrow"),
        P(None, "narrow", None),
        P(None, "narrow", None),
    )
    out_specs = (P(None, "narrow", None), P(None, "narrow", None))
    step = functools.partial(shards, mesh.shape["wide"], mesh.shape["narrow"])
    return jax.shard_map(step, mesh=mesh, in_specs=in_specs, out_specs=out_specs, check_vma=False)
```

time: 43.1 us -> 37.2 us (0.86)
  Pallas kernels: 40.4 us -> 35.5 us
  other arithmetic: 1.85 us -> 0.9 us
    pallas_call x1, Pallas kernels: 40.4 us -> 35.5 us  [shards(): pl.pallas_call(functools.partial(tower_kernel, n_wide, n_narrow, pieces,...]
    sub x1, other arithmetic: 1.85 us -> 0.9 us  [shards(): table - learn_rate * summed / (jnp.sqrt(new_accum) + epsilon)]
where the time goes in v2:
time: 37.2 us; the launch traced here: 37.1 us
  Pallas kernels  35.5 us (95%)
  other arithmetic  0.9 us (2%)
  between operations  0.67 us (2%)
    pallas_call x1, Pallas kernels, shards(): pl.pallas_call(functools.partial(tower_kernel, n_wide, n_narrow, pieces,...  35.5 us
    sub x1, other arithmetic, shards(): table - learn_rate * summed / (jnp.sqrt(new_accum) + epsilon)  0.9 us

profile of v2, /device:TPU:0, one launch (start us, length us, event | category | flops | bytes accessed | tf_op | source)
XLA Modules:
  0.0 37.1 jit_solution(12484680468235157069)
XLA Ops:
  0.6 0.0 copy-start
  0.6 0.0 copy-start.1
  0.7 35.5 %tower.1 = f32[8,64,128]{2,1,0:T(8,128)S(1)} custom-call(bf16[512,1024]{1,0:T(8,128)(2,1)} %pooled_hbm.1, bf16[512,512]{1,0:T(8,128)(2,1)} %cot_hbm.1, bf16[256,1024]{1,0:T(8,128)(2,1)} %w1_hbm.1, bf16[256,512]{1,0:T(8,128)(2,1)} %w2_hbm.1, f32[1,1024]{1,0:T(1,128)} %bitcast.1, bf16[8,16,2048]{2,1,0:T(8,128)(2,1)} %counts_hbm.1, s32[8,16]{1,0:T(8,128)} %ids_hbm.1), custom_call_target="tpu_custom_call" | custom-call | tf_op jit(solution)/shard_map/tower/pallas_call | solution.py:408
  36.1 0.0 copy-done
  36.2 0.0 copy-done.1
  36.2 0.9 %divide_subtract_fusion = (f32[8,64,128]{2,1,0:T(8,128)}, f32[8,64,128]{2,1,0:T(8,128)}) fusion(f32[8,64,128]{2,1,0:T(8,128)S(1)} %copy-done, f32[8,64,128]{2,1,0:T(8,128)S(1)} %tower.1, f32[8,64,128]{2,1,0:T(8,128)S(1)} %copy-done.1), kind=kLoop, calls=%fused_computation | loop fusion | flops 393216 | bytes 1310720 | tf_op jit(solution)/shard_map/sub | solution.py:448
Async XLA Ops:
  0.6 35.5 %copy-start = (f32[8,64,128]{2,1,0:T(8,128)S(1)}, f32[8,64,128]{2,1,0:T(8,128)}, u32[]{:S(2)}) copy-start(f32[8,64,128]{2,1,0:T(8,128)} %param.16) | copy-start | bytes 786436
  0.6 35.5 %copy-start.1 = (f32[8,64,128]{2,1,0:T(8,128)S(1)}, f32[8,64,128]{2,1,0:T(8,128)}, u32[]{:S(2)}) copy-start(f32[8,64,128]{2,1,0:T(8,128)} %param.17) | copy-start | bytes 786436

commit v3 on v2

v3 whole, which is shorter than its diff:
```python
import functools
import math

import jax
import jax.numpy as jnp
from jax import lax
from jax.experimental import pallas as pl
from jax.experimental.pallas import tpu as pltpu
from jax.sharding import PartitionSpec as P

MESH = pl.DeviceIdType.MESH
clip_factor = 0.5
learn_rate = 0.05
epsilon = 1e-08
NT = (((1,), (1,)), ((), ()))
HOP_Z = 3.0
STEP_Z = 0.35
PACE = 0.0
HOP_S = 3.4
HOP_D = 3.4
HOP_C = 1.4
HOP_W = 4.0
STRAIGHT = 1
ACT_TILE = 512
Z_UNITS = ()
HALVES = 2
VMEM_KIB = 32 * 1024


def flip(index, mask):
    bit = 1
    while bit <= mask:
        if mask & bit:
            index = index + bit * (1 - 2 * ((index // bit) % 2))
        bit *= 2
    return index


def pieces_of(shard_rows, n_wide):
    pieces = 1
    while pieces < 8 and n_wide % (2 * pieces) == 0 and shard_rows % (32 * pieces) == 0:
        pieces *= 2
    return pieces


def arrivals(n, n_narrow, count):
    items = []
    for s in range(n_narrow):
        if s != n:
            for v in range(count):
                items.append(((abs(s - n) - 1) * count + v, s > n, s, v))
    return [(s, v) for _, _, s, v in sorted(items)]


def tower_kernel(
    n_wide, n_narrow, pieces, scale, limit,
    pooled_hbm, cot_hbm, w1_hbm, w2_hbm, bias_hbm, counts_hbm, ids_hbm, out_ref,
    pooled, cot, weights, bias, ids, looks, hidden, back, deltas, grad_in, gfull, gsend, grecv, sums,
    local_sem, send_sem, z_sem, x_sem, y_sem, d_sem, c_sem, look_sem, grad_sem, sum_sem,
):
    wide = lax.axis_index("wide")
    narrow = lax.axis_index("narrow")
    shard, inner = w1_hbm.shape
    top = w2_hbm.shape[1]
    units = inner // top + 1
    piece_rows = shard // pieces
    bags = pooled.shape[0]
    emb = gfull.shape[3]
    tables, slots = looks.shape[1], looks.shape[2]
    rest = n_narrow - 1
    part = wide % pieces
    base = wide - part
    has_core, has_x, has_y = pieces >= 2, pieces >= 4, pieces >= 8
    def lane_block(index, size):
        return pl.ds(pl.multiple_of(index * size, size), size)

    def local(step, src, dst):
        return pltpu.make_async_copy(src, dst, local_sem.at[step])

    own_rows = lane_block(narrow, shard)
    own_w = [
        local(0, w1_hbm, weights.at[own_rows, pl.ds(0, inner)]),
        local(1, w2_hbm, weights.at[own_rows, pl.ds(inner, top)]),
    ]
    own_x = [local(2, pooled_hbm, pooled), local(3, cot_hbm, cot)]
    own_rest = [
        local(4, counts_hbm.at[:, :, lane_block(narrow, bags)], looks.at[narrow]),
        local(5, bias_hbm, bias),
        local(6, ids_hbm, ids),
    ]
    for copy in own_w + own_x + own_rest:
        copy.start()

    barrier = pltpu.get_barrier_semaphore()

    def greet(device):
        pl.semaphore_signal(barrier, inc=1, device_id=device, device_id_type=MESH)

    @pl.when(narrow > 0)
    def _():
        greet({"narrow": narrow - 1})

    @pl.when(narrow < n_narrow - 1)
    def _():
        greet({"narrow": narrow + 1})

    if pieces == n_wide:
        beside = [base + flip(part, m) for m in (1, 2, 4) if m < pieces]
    else:
        beside = [(wide + d) % n_wide for d in range(1, n_wide)]
    for device in beside:
        greet({"wide": device})
    ends = jnp.where(narrow > 0, 1, 0) + jnp.where(narrow < n_narrow - 1, 1, 0)
    pl.semaphore_wait(barrier, ends + len(beside))

    def remote(src, dst, recv, device):
        return pltpu.make_async_remote_copy(
            src_ref=src, dst_ref=dst, send_sem=send_sem, recv_sem=recv,
            device_id=device, device_id_type=MESH,
        )

    sent = []

    def launch(copy, cond=None):
        if cond is None:
            copy.start()
        else:
            @pl.when(cond)
            def _():
                copy.start()
        sent.append((copy, cond))

    def pick(values):
        if all(v == values[0] for v in values):
            return values[0]
        total = 0
        for n, v in enumerate(values):
            total = total + jnp.where(narrow == n, v, 0)
        return total

    def slot_of(s, n):
        return (s - n + n_narrow) % n_narrow - 1

    def view(s, q, u):
        rows = pl.ds(pl.multiple_of(s * shard + q * piece_rows, piece_rows), piece_rows)
        return weights.at[rows, lane_block(u, top)]

    crosses = [u for u in range(units) if has_y and n_narrow <= 4 and u in Z_UNITS]

    def piece_of(s, v):
        if crosses and v >= units:
            return view(s, flip(part, 6), crosses[v - units])
        return view(s, part, v)

    for copy in own_w:
        copy.wait()
    for v in range(units + len(crosses)):
        w = piece_of(narrow, v)
        for ahead, cond in ((narrow + 1, narrow < n_narrow - 1), (narrow - 1, narrow > 0)):
            launch(remote(w, w, z_sem.at[slot_of(narrow, ahead), v], {"narrow": ahead}), cond)

    order = [arrivals(n, n_narrow, units + len(crosses)) for n in range(n_narrow)]
    groups = tables // 2
    ranks = [sorted((s for s in range(n_narrow) if s != n), key=lambda s: (abs(s - n), s > n)) for n in range(n_narrow)]

    def await_view(w, sem):
        remote(w, w, sem, {"narrow": (narrow + 1) % n_narrow}).wait_recv()

    class Role:
        def __init__(self, members):
            self.members = members
            self.started = 0
            self.looks = 0

        def item(self, j):
            pairs = [order[n][j] if n in self.members else (-1, -1) for n in range(n_narrow)]
            fill = order[self.members[0]][j]
            pairs = [fill if p[0] < 0 else p for p in pairs]
            s, u = pick([p[0] for p in pairs]), pick([p[1] for p in pairs])
            assert not crosses or isinstance(u, int)
            return s, u, slot_of(s, narrow)

        def send(self, w, sem, device):
            remote(w, w, sem, device).start()
            self.started += 1

        def straight(self, j):
            return has_y and all(order[n][j][0] in ranks[n][rest - STRAIGHT:] for n in self.members) and (
                not crosses or order[self.members[0]][j][1] not in crosses
            )

        def to_core(self, w, slot):
            if has_core:
                self.send(w, c_sem.at[slot], {"wide": base + flip(part, 1)})

        def chain(self, j):
            s, u, slot = self.item(j)
            w = piece_of(s, u)
            await_view(w, z_sem.at[slot, u])
            if 0 not in self.members:
                ahead = jnp.where(s < narrow, narrow + 1, narrow - 1)
                self.send(w, z_sem.at[slot_of(s, ahead), u], {"narrow": ahead})
            if crosses and u >= units:
                self.to_core(w, slot)

        def plane(self, j):
            s, u, slot = self.item(j)
            w = view(s, part, u)
            if has_x:
                self.send(w, x_sem.at[slot, u], {"wide": base + flip(part, 2)})
            if has_y:
                self.send(w, y_sem.at[slot, u], {"wide": base + flip(part, 4)})
            if self.straight(j):
                self.send(w, d_sem.at[slot, u], {"wide": base + flip(part, 6)})
            self.to_core(w, slot)

        def side(self, j):
            s, u, slot = self.item(j)
            odd = (s if crosses else u + jnp.where(u == units - 1, s, 0)) % 2
            for name, mask, sem, there, turn in (("x", 2, x_sem, 4, 0), ("y", 4, y_sem, 2, 1)):
                if mask < pieces:
                    w = view(s, flip(part, mask), u)
                    await_view(w, sem.at[slot, u])
                    if has_y and not (crosses and u in crosses) and not self.straight(j):
                        onward = remote(w, w, d_sem.at[slot, u], {"wide": base + flip(part, there)})

                        @pl.when(odd == turn)
                        def _():
                            onward.start()
                    self.to_core(w, slot)
            if has_y and not (crosses and u in crosses) and not self.straight(j):
                self.started += 1

        def corner(self, j):
            s, u, slot = self.item(j)
            w = view(s, flip(part, 6), u)
            await_view(w, d_sem.at[slot, u])
            self.to_core(w, slot)

        def gathered(self, i):
            s = pick([ranks[n][i] if n in self.members else ranks[self.members[0]][i] for n in range(n_narrow)])
            if has_core:
                await_view(weights.at[pl.ds(0, shard // 2), :], c_sem.at[slot_of(s, narrow)])
            if chunked and i < rest - 1:
                add_chunk(s, False)

        def lookups(self, d):
            for g in range(groups):
                block = pl.ds(2 * g, 2)
                for side in (narrow - d, narrow + d):
                    valid = jnp.logical_and(side >= 0, side < n_narrow)
                    copy = remote(
                        counts_hbm.at[block, :, lane_block(jnp.where(valid, side, 0), bags)],
                        looks.at[narrow, block], look_sem.at[g], {"narrow": jnp.where(valid, side, (narrow + 1) % n_narrow)},
                    )

                    @pl.when(valid)
                    def _():
                        copy.start()

        def settle(self):
            most = weights.shape[0] // piece_rows
            count = self.started
            while count > 0:
                k = min(count, most)
                w = weights.at[pl.ds(0, k * piece_rows), pl.ds(0, top)]
                remote(w, w, c_sem.at[0], {"narrow": (narrow + 1) % n_narrow}).wait_send()
                count -= k

    def add_chunk(source, fresh):
        rows = lane_block(source, shard)
        value = jnp.dot(
            pooled[:, rows], weights[rows, pl.ds(0, inner)], preferred_element_type=jnp.float32
        )
        if fresh:
            hidden[...] = value
        else:
            hidden[...] = hidden[...] + value
        back[:, rows] = lax.dot_general(
            cot[...], weights[rows, pl.ds(inner, top)], NT, preferred_element_type=jnp.float32
        )

    chunked = shard % 128 == 0
    for copy in own_x:
        copy.wait()
    if chunked:
        add_chunk(narrow, True)

    roles = [Role([n for n in (0, n_narrow - 1)])]
    if n_narrow > 2:
        roles.append(Role(list(range(1, n_narrow - 1))))
    for r, role in enumerate(roles):
        n = role.members[0]
        plan = []
        at = {}
        placed = 0
        for j, (s, u) in enumerate(order[n]):
            z = HOP_Z * abs(s - n) + STEP_Z * u
            plan.append((z, 0, role.chain, j))
            last = z
            if u < units:
                p = z if r == 0 else max(z, HOP_Z + PACE * placed)
                if role.straight(j):
                    p = max(p, HOP_Z + HOP_S + 0.01)
                placed += 1
                plan.append((p, 1, role.plane, j))
                last = p
                if has_x:
                    last = p + HOP_S
                    plan.append((last, 2, role.side, j))
                if has_y and u not in crosses:
                    last = p + (HOP_W if role.straight(j) else HOP_S + HOP_D)
                    plan.append((last, 3, role.corner, j))
            at[s] = max(last, at.get(s, 0.0))
        done = max(t for t, _, kind, _ in plan if kind == role.chain)
        for d in range(1, n_narrow):
            early = r == 0 and d == 1
            plan.append((0.0 if early else done, 1.5, role.lookups, d))
        for i in range(rest):
            s = ranks[n][i]
            plan.append((at[s] + HOP_C, 4, role.gathered, i))
        plan.sort(key=lambda e: e[:2])
        kinds = [(e[2], e[3]) for e in plan]
        for j in range(len(order[n])):
            if order[n][j][1] < units and role.straight(j):
                assert kinds.index((role.side, 0)) < kinds.index((role.plane, j))

        @pl.when(jnp.logical_or(narrow == 0, narrow == n_narrow - 1) if r == 0 else jnp.logical_and(narrow > 0, narrow < n_narrow - 1))
        def _():
            for _, _, event, j in plan:
                event(j)

    for copy in own_rest:
        copy.wait()
    tile = min(ACT_TILE, inner)
    if chunked:
        last = lane_block(pick([r[rest - 1] for r in ranks]), shard)
        back[:, last] = lax.dot_general(
            cot[...], weights[last, pl.ds(inner, top)], NT, preferred_element_type=jnp.float32
        )
    for t in range(inner // tile):
        columns = pl.ds(t * tile, tile)
        if chunked:
            value = hidden[:, columns] + jnp.dot(
                pooled[:, last], weights[last, columns], preferred_element_type=jnp.float32
            )
            back_value = back[:, columns]
        else:
            value = jnp.dot(pooled[...], weights[:, columns], preferred_element_type=jnp.float32)
            back_value = lax.dot_general(
                cot[...], weights[columns, pl.ds(inner, top)], NT, preferred_element_type=jnp.float32
            )
        value = value + bias[:, columns]
        sig = jax.nn.sigmoid(value)
        slopes = sig * (1.0 + value * (1.0 - sig))
        deltas[:, columns] = (back_value * slopes).astype(jnp.bfloat16)
    far = [[s for _, s in sorted((-abs(s - n), s) for s in range(n_narrow) if s != n)] for n in range(n_narrow)]
    per_half = groups // HALVES if groups % HALVES == 0 else groups
    for h in range(groups // per_half):
        span = pl.ds(2 * h * per_half * emb, 2 * per_half * emb)
        grad_in[:, span] = lax.dot_general(
            deltas[...], weights[span, pl.ds(0, inner)], NT, preferred_element_type=jnp.float32
        ).astype(jnp.bfloat16)
        for g in range(h * per_half, (h + 1) * per_half):
            await_view(looks.at[pl.ds(0, rest), pl.ds(2 * g, 2)], look_sem.at[g])
        for g in range(h * per_half, (h + 1) * per_half):
            lookups = looks[:, 2 * g:2 * (g + 1)].reshape(n_narrow * 2 * slots, bags)
            value = jnp.dot(
                lookups, grad_in[:, 2 * g * emb:2 * (g + 1) * emb],
                preferred_element_type=jnp.float32,
            )
            value = value.reshape(n_narrow, 2, slots, 2 * emb)
            for i in range(2):
                rows = value[:, i, :, i * emb:(i + 1) * emb]
                gfull[:, 2 * g + i] = rows
                gsend[:, 2 * g + i] = rows.astype(jnp.bfloat16)
        for g in range(h * per_half, (h + 1) * per_half):
            block = pl.ds(2 * g, 2)
            for i in range(rest):
                owner = pick([f[i] for f in far])
                launch(remote(
                    gsend.at[owner, block], grecv.at[slot_of(narrow, owner), block],
                    grad_sem.at[g], {"narrow": owner},
                ))
    for g in range(groups):
        block = pl.ds(2 * g, 2)
        await_view(grecv.at[:, block], grad_sem.at[g])
        total = gfull[narrow, block]
        for d in range(rest):
            total = total + grecv[d, block].astype(jnp.float32)
        grads = total * scale
        norms = jnp.sqrt(jnp.sum(grads * grads, axis=-1, keepdims=True))
        sums[wide, block] = (grads * (limit / jnp.maximum(norms, limit))).astype(jnp.bfloat16)
        for e in range(n_wide - 1, 0, -1):
            peer = base + flip(part, e) if pieces == n_wide else (wide + e) % n_wide
            launch(remote(
                sums.at[wide, block], sums.at[wide, block], sum_sem.at[g], {"wide": peer},
            ))
    for g in range(groups):
        block = pl.ds(2 * g, 2)
        await_view(sums.at[pl.ds(0, n_wide - 1), block], sum_sem.at[g])
        summed = sums[0, block].astype(jnp.float32)
        for q in range(1, n_wide):
            summed = summed + sums[q, block].astype(jnp.float32)
        for i in range(2):
            k = 2 * g + i
            hot = lax.broadcasted_iota(jnp.int32, (out_ref.shape[1], slots), 0) == ids[k:k + 1, :]
            out_ref[k] = jnp.dot(
                hot.astype(jnp.float32), summed[i], precision=lax.Precision.HIGHEST,
                preferred_element_type=jnp.float32,
            )
    for g in range(groups):
        w = looks.at[pl.ds(0, rest), pl.ds(2 * g, 2)]
        remote(w, w, c_sem.at[0], {"narrow": (narrow + 1) % n_narrow}).wait_send()
    for r, role in enumerate(roles):
        @pl.when(jnp.logical_or(narrow == 0, narrow == n_narrow - 1) if r == 0 else jnp.logical_and(narrow > 0, narrow < n_narrow - 1))
        def _():
            role.settle()
    for copy, cond in sent:
        if cond is None:
            copy.wait_send()
        else:
            @pl.when(cond)
            def _():
                copy.wait_send()


def shards(n_wide, n_narrow, pooled, cotangent, w_first, b_first, w_second, counts, row_ids, table, accum):
    tables, slots, group_bags = counts.shape
    emb = table.shape[2]
    bags, emb_all = pooled.shape
    shard, inner = w_first.shape
    top = w_second.shape[1]
    units = inner // top + 1
    pieces = pieces_of(shard, n_wide)
    rest = n_narrow - 1
    groups = tables // 2
    scale = 1.0 / math.sqrt(group_bags)
    limit = clip_factor * math.sqrt(emb)
    hbm = pl.BlockSpec(memory_space=pl.ANY)
    vmem = pl.BlockSpec(memory_space=pltpu.VMEM)
    dma = pltpu.SemaphoreType.DMA
    summed = pl.pallas_call(
        functools.partial(tower_kernel, n_wide, n_narrow, pieces, scale, limit),
        out_shape=jax.ShapeDtypeStruct(table.shape, jnp.float32),
        in_specs=[hbm] * 7,
        out_specs=vmem,
        scratch_shapes=[
            pltpu.VMEM((bags, emb_all), jnp.bfloat16),
            pltpu.VMEM((bags, top), jnp.bfloat16),
            pltpu.VMEM((emb_all, inner + top), jnp.bfloat16),
            pltpu.VMEM((1, inner), jnp.float32),
            pltpu.VMEM(row_ids.shape, jnp.int32),
            pltpu.VMEM((n_narrow, tables, slots, bags), jnp.bfloat16),
            pltpu.VMEM((bags, inner), jnp.float32),
            pltpu.VMEM((bags, inner), jnp.float32),
            pltpu.VMEM((bags, inner), jnp.bfloat16),
            pltpu.VMEM((bags, emb_all), jnp.bfloat16),
            pltpu.VMEM((n_narrow, tables, slots, emb), jnp.float32),
            pltpu.VMEM((n_narrow, tables, slots, emb), jnp.bfloat16),
            pltpu.VMEM((rest, tables, slots, emb), jnp.bfloat16),
            pltpu.VMEM((n_wide, tables, slots, emb), jnp.bfloat16),
            dma((7,)),
            dma,
            dma((rest, units + len(Z_UNITS))),
            dma((rest, units)),
            dma((rest, units)),
            dma((rest, units)),
            dma((rest,)),
            dma((groups,)),
            dma((groups,)),
            dma((groups,)),
        ],
        compiler_params=pltpu.CompilerParams(
            collective_id=0, has_side_effects=True, vmem_limit_bytes=VMEM_KIB * 1024
        ),
        name="tower",
    )(*[
        pltpu.with_memory_space_constraint(x, pltpu.HBM)
        for x in (pooled, cotangent, w_first, w_second, b_first.reshape(1, inner), counts, row_ids)
    ])
    new_accum = accum + summed * summed
    return table - learn_rate * summed / (jnp.sqrt(new_accum) + epsilon), new_accum


def solution(mesh):
    in_specs = (
        P(("wide", "narrow"), None),
        P(("wide", "narrow"), None),
        P("narrow", None),
        P(),
        P("narrow", None),
        P(None, "narrow", "wide"),
        P(None, "narrow"),
        P(None, "narrow", None),
        P(None, "narrow", None),
    )
    out_specs = (P(None, "narrow", None), P(None, "narrow", None))
    step = functools.partial(shards, mesh.shape["wide"], mesh.shape["narrow"])
    return jax.shard_map(step, mesh=mesh, in_specs=in_specs, out_specs=out_specs, check_vma=False)
```

time: 37.2 us -> 35.3 us (0.949)
  Pallas kernels: 35.5 us -> 33.5 us
    pallas_call x1, Pallas kernels: 35.5 us -> 33.5 us  [shards(): pl.pallas_call(functools.partial(tower_kernel, n_wide, n_narrow, pieces,...]
where the time goes in v3:
time: 35.3 us; the launch traced here: 35.1 us
  Pallas kernels  33.5 us (95%)
  other arithmetic  0.9 us (3%)
  between operations  0.67 us (2%)
    pallas_call x1, Pallas kernels, shards(): pl.pallas_call(functools.partial(tower_kernel, n_wide, n_narrow, pieces,...  33.5 us
    sub x1, other arithmetic, shards(): table - learn_rate * summed / (jnp.sqrt(new_accum) + epsilon)  0.9 us

profile of v3, /device:TPU:0, one launch (start us, length us, event | category | flops | bytes accessed | tf_op | source)
XLA Modules:
  0.0 35.1 jit_solution(15459899668928288974)
XLA Ops:
  0.6 0.0 copy-start
  0.6 0.0 copy-start.1
  0.7 33.5 %tower.1 = f32[8,64,128]{2,1,0:T(8,128)S(1)} custom-call(bf16[512,1024]{1,0:T(8,128)(2,1)} %pooled_hbm.1, bf16[512,512]{1,0:T(8,128)(2,1)} %cot_hbm.1, bf16[256,1024]{1,0:T(8,128)(2,1)} %w1_hbm.1, bf16[256,512]{1,0:T(8,128)(2,1)} %w2_hbm.1, f32[1,1024]{1,0:T(1,128)} %bitcast.1, bf16[8,16,2048]{2,1,0:T(8,128)(2,1)} %counts_hbm.1, s32[8,16]{1,0:T(8,128)} %ids_hbm.1), custom_call_target="tpu_custom_call" | custom-call | tf_op jit(solution)/shard_map/tower/pallas_call | solution.py:443
  34.2 0.0 copy-done
  34.2 0.0 copy-done.1
  34.2 0.9 %divide_subtract_fusion = (f32[8,64,128]{2,1,0:T(8,128)}, f32[8,64,128]{2,1,0:T(8,128)}) fusion(f32[8,64,128]{2,1,0:T(8,128)S(1)} %copy-done, f32[8,64,128]{2,1,0:T(8,128)S(1)} %tower.1, f32[8,64,128]{2,1,0:T(8,128)S(1)} %copy-done.1), kind=kLoop, calls=%fused_computation | loop fusion | flops 393216 | bytes 1310720 | tf_op jit(solution)/shard_map/sub | solution.py:483
Async XLA Ops:
  0.6 33.6 %copy-start = (f32[8,64,128]{2,1,0:T(8,128)S(1)}, f32[8,64,128]{2,1,0:T(8,128)}, u32[]{:S(2)}) copy-start(f32[8,64,128]{2,1,0:T(8,128)} %param.16) | copy-start | bytes 786436
  0.6 33.6 %copy-start.1 = (f32[8,64,128]{2,1,0:T(8,128)S(1)}, f32[8,64,128]{2,1,0:T(8,128)}, u32[]{:S(2)}) copy-start(f32[8,64,128]{2,1,0:T(8,128)} %param.17) | copy-start | bytes 786436

commit v4 on v3

--- a/solution.py
+++ b/solution.py
@@ -21,8 +21,13 @@
 HOP_C = 1.4
 HOP_W = 4.0
 STRAIGHT = 1
+END_2 = 0.0
+END_3 = 0.0
+MID_0 = 0.0
+MID_1 = -2.6
+MID_2 = 0.0
 ACT_TILE = 512
-Z_UNITS = ()
+Z_UNITS = (2,)
 HALVES = 2
 VMEM_KIB = 32 * 1024
 
@@ -244,19 +249,23 @@
             if chunked and i < rest - 1:
                 add_chunk(s, False)
 
-        def lookups(self, d):
+        def lookups(self, way):
+            d, inner = way
+            middle = narrow < n_narrow - 1 - narrow
+            up = middle if inner else jnp.logical_not(middle)
+            owner = jnp.where(up, narrow + d, narrow - d)
+            valid = jnp.logical_and(owner >= 0, owner < n_narrow)
+            owner = jnp.where(valid, owner, (narrow + 1) % n_narrow)
             for g in range(groups):
                 block = pl.ds(2 * g, 2)
-                for side in (narrow - d, narrow + d):
-                    valid = jnp.logical_and(side >= 0, side < n_narrow)
-                    copy = remote(
-                        counts_hbm.at[block, :, lane_block(jnp.where(valid, side, 0), bags)],
-                        looks.at[narrow, block], look_sem.at[g], {"narrow": jnp.where(valid, side, (narrow + 1) % n_narrow)},
-                    )
-
-                    @pl.when(valid)
-                    def _():
-                        copy.start()
+                copy = remote(
+                    counts_hbm.at[block, :, lane_block(owner, bags)], looks.at[narrow, block],
+                    look_sem.at[g], {"narrow": owner},
+                )
+
+                @pl.when(valid)
+                def _():
+                    copy.start()
 
         def settle(self):
             most = weights.shape[0] // piece_rows
@@ -314,8 +323,11 @@
             at[s] = max(last, at.get(s, 0.0))
         done = max(t for t, _, kind, _ in plan if kind == role.chain)
         for d in range(1, n_narrow):
-            early = r == 0 and d == 1
-            plan.append((0.0 if early else done, 1.5, role.lookups, d))
+            if r == 0:
+                plan.append((0.0 if d == 1 else done + (END_2 if d == 2 else END_3), 1.5, role.lookups, (d, True)))
+            else:
+                plan.append((done + (MID_1 if d == 1 else MID_2), 1.5, role.lookups, (d, True)))
+                plan.append((done + MID_0, 1.5, role.lookups, (d, False)))
         for i in range(rest):
             s = ranks[n][i]
             plan.append((at[s] + HOP_C, 4, role.gathered, i))

time: 35.3 us -> 34.6 us (0.980)
  Pallas kernels: 33.5 us -> 32.9 us
    pallas_call x1, Pallas kernels: 33.5 us -> 32.9 us  [shards(): pl.pallas_call(functools.partial(tower_kernel, n_wide, n_narrow, pieces,...]
where the time goes in v4:
time: 34.6 us; the launch traced here: 34.5 us
  Pallas kernels  32.9 us (95%)
  other arithmetic  0.9 us (3%)
  between operations  0.67 us (2%)
    pallas_call x1, Pallas kernels, shards(): pl.pallas_call(functools.partial(tower_kernel, n_wide, n_narrow, pieces,...  32.9 us
    sub x1, other arithmetic, shards(): table - learn_rate * summed / (jnp.sqrt(new_accum) + epsilon)  0.9 us

profile of v4, /device:TPU:0, one launch (start us, length us, event | category | flops | bytes accessed | tf_op | source)
XLA Modules:
  0.0 34.5 jit_solution(10713829725353958405)
XLA Ops:
  0.6 0.0 copy-start
  0.6 0.0 copy-start.1
  0.7 32.9 %tower.1 = f32[8,64,128]{2,1,0:T(8,128)S(1)} custom-call(bf16[512,1024]{1,0:T(8,128)(2,1)} %pooled_hbm.1, bf16[512,512]{1,0:T(8,128)(2,1)} %cot_hbm.1, bf16[256,1024]{1,0:T(8,128)(2,1)} %w1_hbm.1, bf16[256,512]{1,0:T(8,128)(2,1)} %w2_hbm.1, f32[1,1024]{1,0:T(1,128)} %bitcast.1, bf16[8,16,2048]{2,1,0:T(8,128)(2,1)} %counts_hbm.1, s32[8,16]{1,0:T(8,128)} %ids_hbm.1), custom_call_target="tpu_custom_call" | custom-call | tf_op jit(solution)/shard_map/tower/pallas_call | solution.py:455
  33.6 0.0 copy-done
  33.6 0.0 copy-done.1
  33.6 0.9 %divide_subtract_fusion = (f32[8,64,128]{2,1,0:T(8,128)}, f32[8,64,128]{2,1,0:T(8,128)}) fusion(f32[8,64,128]{2,1,0:T(8,128)S(1)} %copy-done, f32[8,64,128]{2,1,0:T(8,128)S(1)} %tower.1, f32[8,64,128]{2,1,0:T(8,128)S(1)} %copy-done.1), kind=kLoop, calls=%fused_computation | loop fusion | flops 393216 | bytes 1310720 | tf_op jit(solution)/shard_map/sub | solution.py:495
Async XLA Ops:
  0.6 32.9 %copy-start = (f32[8,64,128]{2,1,0:T(8,128)S(1)}, f32[8,64,128]{2,1,0:T(8,128)}, u32[]{:S(2)}) copy-start(f32[8,64,128]{2,1,0:T(8,128)} %param.16) | copy-start | bytes 786436
  0.6 32.9 %copy-start.1 = (f32[8,64,128]{2,1,0:T(8,128)S(1)}, f32[8,64,128]{2,1,0:T(8,128)}, u32[]{:S(2)}) copy-start(f32[8,64,128]{2,1,0:T(8,128)} %param.17) | copy-start | bytes 786436

commit v5 on v4

--- a/solution.py
+++ b/solution.py
@@ -14,7 +14,8 @@
 epsilon = 1e-08
 NT = (((1,), (1,)), ((), ()))
 HOP_Z = 3.0
-STEP_Z = 0.35
+STEP_Z = 0.35 / 2
+SPLIT = 2
 PACE = 0.0
 HOP_S = 3.4
 HOP_D = 3.4
@@ -27,7 +28,7 @@
 MID_1 = -2.6
 MID_2 = 0.0
 ACT_TILE = 512
-Z_UNITS = (2,)
+Z_UNITS = (5,)
 HALVES = 2
 VMEM_KIB = 32 * 1024
 
@@ -61,13 +62,14 @@
     n_wide, n_narrow, pieces, scale, limit,
     pooled_hbm, cot_hbm, w1_hbm, w2_hbm, bias_hbm, counts_hbm, ids_hbm, out_ref,
     pooled, cot, weights, bias, ids, looks, hidden, back, deltas, grad_in, gfull, gsend, grecv, sums,
-    local_sem, send_sem, z_sem, x_sem, y_sem, d_sem, c_sem, look_sem, grad_sem, sum_sem,
+    local_sem, send_sem, z_sem, side_sem, d_sem, c_sem, look_sem, grad_sem, sum_sem,
 ):
     wide = lax.axis_index("wide")
     narrow = lax.axis_index("narrow")
     shard, inner = w1_hbm.shape
     top = w2_hbm.shape[1]
-    units = inner // top + 1
+    width = top // SPLIT
+    units = (inner + top) // width
     piece_rows = shard // pieces
     bags = pooled.shape[0]
     emb = gfull.shape[3]
@@ -148,7 +150,7 @@
 
     def view(s, q, u):
         rows = pl.ds(pl.multiple_of(s * shard + q * piece_rows, piece_rows), piece_rows)
-        return weights.at[rows, lane_block(u, top)]
+        return weights.at[rows, lane_block(u, width)]
 
     crosses = [u for u in range(units) if has_y and n_narrow <= 4 and u in Z_UNITS]
 
@@ -212,20 +214,21 @@
             s, u, slot = self.item(j)
             w = view(s, part, u)
             if has_x:
-                self.send(w, x_sem.at[slot, u], {"wide": base + flip(part, 2)})
+                self.send(w, side_sem.at[slot, u], {"wide": base + flip(part, 2)})
             if has_y:
-                self.send(w, y_sem.at[slot, u], {"wide": base + flip(part, 4)})
+                self.send(w, side_sem.at[slot, u], {"wide": base + flip(part, 4)})
             if self.straight(j):
                 self.send(w, d_sem.at[slot, u], {"wide": base + flip(part, 6)})
             self.to_core(w, slot)
 
         def side(self, j):
             s, u, slot = self.item(j)
-            odd = (s if crosses else u + jnp.where(u == units - 1, s, 0)) % 2
-            for name, mask, sem, there, turn in (("x", 2, x_sem, 4, 0), ("y", 4, y_sem, 2, 1)):
+            odd = (s + u if crosses else u + jnp.where(u == units - 1, s, 0)) % 2
+            beside = 2 if has_y else 1
+            await_view(weights.at[pl.ds(0, beside * piece_rows), lane_block(u, width)], side_sem.at[slot, u])
+            for mask, there, turn in ((2, 4, 0), (4, 2, 1)):
                 if mask < pieces:
                     w = view(s, flip(part, mask), u)
-                    await_view(w, sem.at[slot, u])
                     if has_y and not (crosses and u in crosses) and not self.straight(j):
                         onward = remote(w, w, d_sem.at[slot, u], {"wide": base + flip(part, there)})
 
@@ -272,7 +275,7 @@
             count = self.started
             while count > 0:
                 k = min(count, most)
-                w = weights.at[pl.ds(0, k * piece_rows), pl.ds(0, top)]
+                w = weights.at[pl.ds(0, k * piece_rows), pl.ds(0, width)]
                 remote(w, w, c_sem.at[0], {"narrow": (narrow + 1) % n_narrow}).wait_send()
                 count -= k
 
@@ -443,7 +446,8 @@
     bags, emb_all = pooled.shape
     shard, inner = w_first.shape
     top = w_second.shape[1]
-    units = inner // top + 1
+    width = top // SPLIT
+    units = (inner + top) // width
     pieces = pieces_of(shard, n_wide)
     rest = n_narrow - 1
     groups = tables // 2
@@ -477,7 +481,6 @@
             dma((rest, units + len(Z_UNITS))),
             dma((rest, units)),
             dma((rest, units)),
-            dma((rest, units)),
             dma((rest,)),
             dma((groups,)),
             dma((groups,)),

time: 34.6 us -> 34 us (0.983)
  Pallas kernels: 32.9 us -> 32.2 us
    pallas_call x1, Pallas kernels: 32.9 us -> 32.2 us  [shards(): pl.pallas_call(functools.partial(tower_kernel, n_wide, n_narrow, pieces,...]
where the time goes in v5:
time: 34 us; the launch traced here: 33.8 us
  Pallas kernels  32.2 us (95%)
  other arithmetic  0.9 us (3%)
  between operations  0.67 us (2%)
    pallas_call x1, Pallas kernels, shards(): pl.pallas_call(functools.partial(tower_kernel, n_wide, n_narrow, pieces,...  32.2 us
    sub x1, other arithmetic, shards(): table - learn_rate * summed / (jnp.sqrt(new_accum) + epsilon)  0.9 us

profile of v5, /device:TPU:0, one launch (start us, length us, event | category | flops | bytes accessed | tf_op | source)
XLA Modules:
  0.0 33.8 jit_solution(6978047139124401629)
XLA Ops:
  0.6 0.0 copy-start
  0.6 0.0 copy-start.1
  0.7 32.2 %tower.1 = f32[8,64,128]{2,1,0:T(8,128)S(1)} custom-call(bf16[512,1024]{1,0:T(8,128)(2,1)} %pooled_hbm.1, bf16[512,512]{1,0:T(8,128)(2,1)} %cot_hbm.1, bf16[256,1024]{1,0:T(8,128)(2,1)} %w1_hbm.1, bf16[256,512]{1,0:T(8,128)(2,1)} %w2_hbm.1, f32[1,1024]{1,0:T(1,128)} %bitcast.1, bf16[8,16,2048]{2,1,0:T(8,128)(2,1)} %counts_hbm.1, s32[8,16]{1,0:T(8,128)} %ids_hbm.1), custom_call_target="tpu_custom_call" | custom-call | tf_op jit(solution)/shard_map/tower/pallas_call | solution.py:459
  32.9 0.0 copy-done
  32.9 0.0 copy-done.1
  32.9 0.9 %divide_subtract_fusion = (f32[8,64,128]{2,1,0:T(8,128)}, f32[8,64,128]{2,1,0:T(8,128)}) fusion(f32[8,64,128]{2,1,0:T(8,128)S(1)} %copy-done, f32[8,64,128]{2,1,0:T(8,128)S(1)} %tower.1, f32[8,64,128]{2,1,0:T(8,128)S(1)} %copy-done.1), kind=kLoop, calls=%fused_computation | loop fusion | flops 393216 | bytes 1310720 | tf_op jit(solution)/shard_map/sub | solution.py:498
Async XLA Ops:
  0.6 32.3 %copy-start = (f32[8,64,128]{2,1,0:T(8,128)S(1)}, f32[8,64,128]{2,1,0:T(8,128)}, u32[]{:S(2)}) copy-start(f32[8,64,128]{2,1,0:T(8,128)} %param.16) | copy-start | bytes 786436
  0.6 32.3 %copy-start.1 = (f32[8,64,128]{2,1,0:T(8,128)S(1)}, f32[8,64,128]{2,1,0:T(8,128)}, u32[]{:S(2)}) copy-start(f32[8,64,128]{2,1,0:T(8,128)} %param.17) | copy-start | bytes 786436

commit v6 on v5

--- a/solution.py
+++ b/solution.py
@@ -20,14 +20,14 @@
 HOP_S = 3.4
 HOP_D = 3.4
 HOP_C = 1.4
-HOP_W = 4.0
+HOP_W = 3.4
 STRAIGHT = 1
 END_2 = 0.0
 END_3 = 0.0
 MID_0 = 0.0
 MID_1 = -2.6
 MID_2 = 0.0
-ACT_TILE = 512
+ACT_TILE = 1024
 Z_UNITS = (5,)
 HALVES = 2
 VMEM_KIB = 32 * 1024

time: 34 us -> 33.9 us (level)
  no operation moved by 1% of the time
where the time goes in v6:
time: 33.9 us; the launch traced here: 33.8 us
  Pallas kernels  32.2 us (95%)
  other arithmetic  0.9 us (3%)
  between operations  0.67 us (2%)
    pallas_call x1, Pallas kernels, shards(): pl.pallas_call(functools.partial(tower_kernel, n_wide, n_narrow, pieces,...  32.2 us
    sub x1, other arithmetic, shards(): table - learn_rate * summed / (jnp.sqrt(new_accum) + epsilon)  0.9 us

profile of v6, /device:TPU:0, one launch (start us, length us, event | category | flops | bytes accessed | tf_op | source)
XLA Modules:
  0.0 33.8 jit_solution(2771226463636671743)
XLA Ops:
  0.6 0.0 copy-start
  0.6 0.0 copy-start.1
  0.7 32.2 %tower.1 = f32[8,64,128]{2,1,0:T(8,128)S(1)} custom-call(bf16[512,1024]{1,0:T(8,128)(2,1)} %pooled_hbm.1, bf16[512,512]{1,0:T(8,128)(2,1)} %cot_hbm.1, bf16[256,1024]{1,0:T(8,128)(2,1)} %w1_hbm.1, bf16[256,512]{1,0:T(8,128)(2,1)} %w2_hbm.1, f32[1,1024]{1,0:T(1,128)} %bitcast.1, bf16[8,16,2048]{2,1,0:T(8,128)(2,1)} %counts_hbm.1, s32[8,16]{1,0:T(8,128)} %ids_hbm.1), custom_call_target="tpu_custom_call" | custom-call | tf_op jit(solution)/shard_map/tower/pallas_call | solution.py:459
  32.8 0.0 copy-done
  32.8 0.0 copy-done.1
  32.9 0.9 %divide_subtract_fusion = (f32[8,64,128]{2,1,0:T(8,128)}, f32[8,64,128]{2,1,0:T(8,128)}) fusion(f32[8,64,128]{2,1,0:T(8,128)S(1)} %copy-done, f32[8,64,128]{2,1,0:T(8,128)S(1)} %tower.1, f32[8,64,128]{2,1,0:T(8,128)S(1)} %copy-done.1), kind=kLoop, calls=%fused_computation | loop fusion | flops 393216 | bytes 1310720 | tf_op jit(solution)/shard_map/sub | solution.py:498
Async XLA Ops:
  0.6 32.2 %copy-start = (f32[8,64,128]{2,1,0:T(8,128)S(1)}, f32[8,64,128]{2,1,0:T(8,128)}, u32[]{:S(2)}) copy-start(f32[8,64,128]{2,1,0:T(8,128)} %param.16) | copy-start | bytes 786436
  0.6 32.2 %copy-start.1 = (f32[8,64,128]{2,1,0:T(8,128)S(1)}, f32[8,64,128]{2,1,0:T(8,128)}, u32[]{:S(2)}) copy-start(f32[8,64,128]{2,1,0:T(8,128)} %param.17) | copy-start | bytes 786436

commit v7 on v6

--- a/solution.py
+++ b/solution.py
@@ -25,7 +25,7 @@
 END_2 = 0.0
 END_3 = 0.0
 MID_0 = 0.0
-MID_1 = -2.6
+MID_1 = -2.0
 MID_2 = 0.0
 ACT_TILE = 1024
 Z_UNITS = (5,)

time: 33.9 us -> 33.9 us (level)
  no operation moved by 1% of the time
where the time goes in v7:
time: 33.9 us; the launch traced here: 33.8 us
  Pallas kernels  32.2 us (95%)
  other arithmetic  0.9 us (3%)
  between operations  0.67 us (2%)
    pallas_call x1, Pallas kernels, shards(): pl.pallas_call(functools.partial(tower_kernel, n_wide, n_narrow, pieces,...  32.2 us
    sub x1, other arithmetic, shards(): table - learn_rate * summed / (jnp.sqrt(new_accum) + epsilon)  0.9 us

profile of v7, /device:TPU:0, one launch (start us, length us, event | category | flops | bytes accessed | tf_op | source)
XLA Modules:
  0.0 33.8 jit_solution(2771226463636671743)
XLA Ops:
  0.6 0.0 copy-start
  0.6 0.0 copy-start.1
  0.7 32.2 %tower.1 = f32[8,64,128]{2,1,0:T(8,128)S(1)} custom-call(bf16[512,1024]{1,0:T(8,128)(2,1)} %pooled_hbm.1, bf16[512,512]{1,0:T(8,128)(2,1)} %cot_hbm.1, bf16[256,1024]{1,0:T(8,128)(2,1)} %w1_hbm.1, bf16[256,512]{1,0:T(8,128)(2,1)} %w2_hbm.1, f32[1,1024]{1,0:T(1,128)} %bitcast.1, bf16[8,16,2048]{2,1,0:T(8,128)(2,1)} %counts_hbm.1, s32[8,16]{1,0:T(8,128)} %ids_hbm.1), custom_call_target="tpu_custom_call" | custom-call | tf_op jit(solution)/shard_map/tower/pallas_call | solution.py:459
  32.8 0.0 copy-done
  32.8 0.0 copy-done.1
  32.9 0.9 %divide_subtract_fusion = (f32[8,64,128]{2,1,0:T(8,128)}, f32[8,64,128]{2,1,0:T(8,128)}) fusion(f32[8,64,128]{2,1,0:T(8,128)S(1)} %copy-done, f32[8,64,128]{2,1,0:T(8,128)S(1)} %tower.1, f32[8,64,128]{2,1,0:T(8,128)S(1)} %copy-done.1), kind=kLoop, calls=%fused_computation | loop fusion | flops 393216 | bytes 1310720 | tf_op jit(solution)/shard_map/sub | solution.py:498
Async XLA Ops:
  0.6 32.2 %copy-start = (f32[8,64,128]{2,1,0:T(8,128)S(1)}, f32[8,64,128]{2,1,0:T(8,128)}, u32[]{:S(2)}) copy-start(f32[8,64,128]{2,1,0:T(8,128)} %param.16) | copy-start | bytes 786436
  0.6 32.2 %copy-start.1 = (f32[8,64,128]{2,1,0:T(8,128)S(1)}, f32[8,64,128]{2,1,0:T(8,128)}, u32[]{:S(2)}) copy-start(f32[8,64,128]{2,1,0:T(8,128)} %param.17) | copy-start | bytes 786436
